TPU v7x, 32 devices: a whole 2x2x4 slice. The times are simulated.
32 devices in a mesh: blk: 8 (over z, y), uly: 4 (over x, core).
Axes of the slice: x: 2, y: 2, z: 4, core: 2. Of those that a mesh axis runs over, the one named last changes fastest.
Arguments:
- tokens: bfloat16 [6400, 1024], P(('blk', 'uly')), may hold values from -6 to 6
- cotangent: bfloat16 [6400, 1024], P(('blk', 'uly')), may hold values from -6 to 6
- noise_embed: bfloat16 [64, 1024], P(('blk', 'uly')), may hold values from -6 to 6
- frame_clip: int32 [64], replicated, may hold values from 0 to 8, as said below
- frame_index: int32 [64], replicated, may hold values from 0 to 31, as said below
- mod_weight: bfloat16 [1024, 6144], replicated, may hold values from -0.1875 to 0.1875
- mod_bias: bfloat16 [6144], replicated, may hold values from -3 to 3
- attn_weight: bfloat16 [1024, 3072], replicated, may hold values from -0.1875 to 0.1875
- attn_bias: bfloat16 [3072], replicated, may hold values from -3 to 3
- proj_weight: bfloat16 [1024, 1024], replicated, may hold values from -3 to 3
- proj_bias: bfloat16 [1024], replicated, may hold values from -3 to 3
- up_weight: bfloat16 [1024, 4096], replicated, may hold values from -0.1875 to 0.1875
- up_bias: bfloat16 [4096], replicated, may hold values from -3 to 3
- down_weight: bfloat16 [4096, 1024], replicated, may hold values from -0.09375 to 0.09375
- down_bias: bfloat16 [1024], replicated, may hold values from -3 to 3
Outputs:
- output: bfloat16 [6400, 1024], P(('blk', 'uly'))
- token_grad: float32 [6400, 1024], P(('blk', 'uly'))
- grad_mod_weight: float32 [1024, 6144], P(('blk', 'uly'))
- grad_mod_bias: float32 [6144], P(('blk', 'uly'))
- grad_attn_weight: float32 [1024, 3072], P(('blk', 'uly'))
- grad_attn_bias: float32 [3072], P(('blk', 'uly'))
- grad_proj_weight: float32 [1024, 1024], P(('blk', 'uly'))
- grad_proj_bias: float32 [1024], P(('blk', 'uly'))
- grad_up_weight: float32 [1024, 4096], P(('blk', 'uly'))
- grad_up_bias: float32 [4096], P(('blk', 'uly'))
- grad_down_weight: float32 [4096, 1024], P(('blk', 'uly'))
- grad_down_bias: float32 [1024], P(('blk', 'uly'))
Inputs may be any that keep to these rules, and one draw needn't show every extreme that they name: `frame_clip`: block b holds frames b * 8 to (b + 1) * 8 - 1. Of these, 4 consecutive frames, either the first or the last ones of the block, form one short clip with id b, and the other 4 frames belong to the one long clip, whose id is the number of blocks and which has frames in every block, 32 in all. `frame_index`: the frame's place within its clip, counting from 0 at the clip's first frame; the long clip's places rise with the frame number.
All inputs are finite; a program needn't handle non-finite values.
Results may differ from a plain program's by a relative error of at most 0.015.
The roundings to bfloat16 on the way count: a program that leaves them out, or rounds other values in their place, can miss the bound.
Values may be sent and summed in bfloat16 or wider, within the bound.
No kernel may reach another device: no remote copies, remote signals or barrier semaphores. Data moves between devices by JAX's collectives and lax.ppermute only.
A program may use at most 320 MiB of HBM per device.

v0:
```python
import math
import jax
import jax.numpy as jnp
from jax import lax
from jax.sharding import PartitionSpec as P

DH = 64
GRID = 10
FB = 8
PATCH = 100
GELU_C = 0.7978845608028654
GELU_K = 0.044715
NEG_BIG = -1e30


def layer_norm(values):
    center = values - jnp.mean(values, axis=-1, keepdims=True)
    inv_std = lax.rsqrt(jnp.mean(center * center, axis=-1, keepdims=True) + 1e-06)
    return (center * inv_std, inv_std)


def norm_back(grad, normed, inv_std):
    return inv_std * (
        grad
        - jnp.mean(grad, axis=-1, keepdims=True)
        - normed * jnp.mean(grad * normed, axis=-1, keepdims=True)
    )


def rope_table(time_pos, row_pos, col_pos):
    half = DH // 2
    n_time = DH // 8
    n_row = 3 * DH // 16
    pair = jnp.arange(half, dtype=jnp.int32)
    in_time = pair < n_time
    in_row = (pair >= n_time) & (pair < n_time + n_row)
    local = jnp.where(in_time, pair, jnp.where(in_row, pair - n_time, pair - n_time - n_row))
    total = jnp.where(in_time, n_time, n_row)
    frequency = jnp.exp(-math.log(10000.0) * local.astype(jnp.float32) / total.astype(jnp.float32))
    place = jnp.where(
        in_time[None, :],
        time_pos[:, None],
        jnp.where(in_row[None, :], row_pos[:, None], col_pos[:, None]),
    )
    angle = place.astype(jnp.float32) * frequency[None, :]
    return (jnp.cos(angle), jnp.sin(angle))


def rotate(values, cosine, sine, sign):
    rows = values.shape[0]
    pairs = values.reshape(rows, -1, DH // 2, 2)
    first = pairs[..., 0]
    second = pairs[..., 1]
    cos_part = cosine[:, None, :]
    sin_part = sign * sine[:, None, :]
    turned = jnp.stack(
        [first * cos_part - second * sin_part, first * sin_part + second * cos_part], axis=-1
    )
    return turned.reshape(values.shape)


def on_device(
    tokens,
    cotangent,
    noise_embed,
    frame_clip,
    frame_index,
    mod_weight,
    mod_bias,
    attn_weight,
    attn_bias,
    proj_weight,
    proj_bias,
    up_weight,
    up_bias,
    down_weight,
    down_bias,
):
    n_uly = lax.axis_size("uly")
    n_blk = lax.axis_size("blk")
    blk_index = lax.axis_index("blk")
    uly_index = lax.axis_index("uly")
    tok_dev, width = tokens.shape
    frames_dev = noise_embed.shape[0]
    block_tok = tok_dev * n_uly
    head_cols = width // n_uly
    heads_dev = head_cols // DH
    scale = 1.0 / math.sqrt(DH)
    patch = jnp.arange(PATCH, dtype=jnp.int32)
    row_of = patch // GRID
    col_of = patch % GRID
    block_clip = lax.dynamic_slice_in_dim(frame_clip, blk_index * FB, FB)
    block_time = lax.dynamic_slice_in_dim(frame_index, blk_index * FB, FB)
    own_time = lax.dynamic_slice_in_dim(block_time, uly_index * frames_dev, frames_dev)
    cos_own, sin_own = rope_table(
        jnp.repeat(own_time, PATCH), jnp.tile(row_of, frames_dev), jnp.tile(col_of, frames_dev)
    )
    cos_blk, sin_blk = rope_table(
        jnp.repeat(block_time, PATCH), jnp.tile(row_of, FB), jnp.tile(col_of, FB)
    )
    silu_noise = jax.nn.silu(noise_embed.astype(jnp.float32)).astype(jnp.bfloat16)
    mod = jnp.dot(silu_noise, mod_weight, preferred_element_type=jnp.float32) + mod_bias.astype(
        jnp.float32
    )
    shift1, scale1, gate1, shift2, scale2, gate2 = [
        mod[:, None, j * width : (j + 1) * width] for j in range(6)
    ]
    framed = tokens.astype(jnp.float32).reshape(frames_dev, PATCH, width)
    normed1, inv_std1 = layer_norm(framed)
    hidden1 = (normed1 * (1.0 + scale1) + shift1).astype(jnp.bfloat16).reshape(tok_dev, width)
    qkv = jnp.dot(hidden1, attn_weight, preferred_element_type=jnp.float32) + attn_bias.astype(
        jnp.float32
    )
    q_tok = rotate(qkv[:, :width], cos_own, sin_own, 1.0).astype(jnp.bfloat16)
    k_tok = rotate(qkv[:, width : 2 * width], cos_own, sin_own, 1.0).astype(jnp.bfloat16)
    v_tok = qkv[:, 2 * width :].astype(jnp.bfloat16)
    q_heads, k_heads, v_heads = (
        lax.all_to_all(q_tok, "uly", split_axis=1, concat_axis=0, tiled=True),
        lax.all_to_all(k_tok, "uly", split_axis=1, concat_axis=0, tiled=True),
        lax.all_to_all(v_tok, "uly", split_axis=1, concat_axis=0, tiled=True),
    )
    k_every, v_every = (
        lax.all_gather(k_heads, "blk", axis=0, tiled=True),
        lax.all_gather(v_heads, "blk", axis=0, tiled=True),
    )
    group = 2
    n_pieces = n_blk // group
    piece_rows = group * block_tok
    key_pieces = k_every.reshape(n_pieces, piece_rows, heads_dev, DH)
    value_pieces = v_every.reshape(n_pieces, piece_rows, heads_dev, DH)
    clip_pieces = jnp.repeat(frame_clip, PATCH).reshape(n_pieces, piece_rows)
    time_pieces = jnp.repeat(frame_index, PATCH).reshape(n_pieces, piece_rows)
    query_clip = jnp.repeat(block_clip, PATCH)
    query_time = jnp.repeat(block_time, PATCH)
    queries = q_heads.reshape(block_tok, heads_dev, DH)

    def piece_score(k_rows, clip_k, time_k):
        allowed = (query_clip[:, None] == clip_k[None, :]) & (
            time_k[None, :] <= query_time[:, None]
        )
        score = (
            jnp.einsum("qhd,khd->hqk", queries, k_rows, preferred_element_type=jnp.float32) * scale
        )
        return (allowed, jnp.where(allowed[None], score, NEG_BIG))

    def gather_stats(carry, pieces):
        top, total = carry
        k_rows, clip_k, time_k = pieces
        allowed, score = piece_score(k_rows, clip_k, time_k)
        new_top = jnp.maximum(top, jnp.max(score, axis=-1))
        expo = jnp.where(allowed[None], jnp.exp(score - new_top[..., None]), 0.0)
        total = total * jnp.exp(top - new_top) + jnp.sum(expo, axis=-1)
        return ((new_top, total), None)

    start_top = jnp.full((heads_dev, block_tok), NEG_BIG, jnp.float32)
    start_total = jnp.zeros((heads_dev, block_tok), jnp.float32)
    (top_all, total_all), _ = lax.scan(
        gather_stats, (start_top, start_total), (key_pieces, clip_pieces, time_pieces)
    )
    log_total = top_all + jnp.log(total_all)

    def mix_values(carry, pieces):
        acc_low, acc_exact = carry
        k_rows, v_rows, clip_k, time_k = pieces
        allowed, score = piece_score(k_rows, clip_k, time_k)
        prob = jnp.where(allowed[None], jnp.exp(score - log_total[..., None]), 0.0)
        acc_low = acc_low + jnp.einsum(
            "hqk,khd->qhd", prob.astype(jnp.bfloat16), v_rows, preferred_element_type=jnp.float32
        )
        acc_exact = acc_exact + jnp.einsum(
            "hqk,khd->qhd", prob, v_rows.astype(jnp.float32), preferred_element_type=jnp.float32
        )
        return ((acc_low, acc_exact), None)

    zero_rows = jnp.zeros((block_tok, heads_dev, DH), jnp.float32)
    (mixed_low, mixed_exact), _ = lax.scan(
        mix_values, (zero_rows, zero_rows), (key_pieces, value_pieces, clip_pieces, time_pieces)
    )
    attn_heads = mixed_low.reshape(block_tok, head_cols).astype(jnp.bfloat16)
    attn_tok = lax.all_to_all(attn_heads, "uly", split_axis=0, concat_axis=1, tiled=True)
    branch = (
        jnp.dot(attn_tok, proj_weight, preferred_element_type=jnp.float32)
        + proj_bias.astype(jnp.float32)
    ).reshape(frames_dev, PATCH, width)
    resid = framed + gate1 * branch
    normed2, inv_std2 = layer_norm(resid)
    hidden2 = (normed2 * (1.0 + scale2) + shift2).astype(jnp.bfloat16).reshape(tok_dev, width)
    pre = jnp.dot(hidden2, up_weight, preferred_element_type=jnp.float32) + up_bias.astype(
        jnp.float32
    )
    inner_tanh = jnp.tanh(GELU_C * (pre + GELU_K * pre * pre * pre))
    act = (0.5 * pre * (1.0 + inner_tanh)).astype(jnp.bfloat16)
    mlp = (
        jnp.dot(act, down_weight, preferred_element_type=jnp.float32)
        + down_bias.astype(jnp.float32)
    ).reshape(frames_dev, PATCH, width)
    output = (resid + gate2 * mlp).reshape(tok_dev, width).astype(jnp.bfloat16)
    dy_grad = cotangent.astype(jnp.float32).reshape(frames_dev, PATCH, width)
    gate2_grad = jnp.sum(dy_grad * mlp, axis=1)
    mlp_grad = (gate2 * dy_grad).astype(jnp.bfloat16).reshape(tok_dev, width)
    g_down_weight = jnp.einsum("tf,td->fd", act, mlp_grad, preferred_element_type=jnp.float32)
    g_down_bias = jnp.sum(mlp_grad.astype(jnp.float32), axis=0)
    act_grad = jnp.einsum("td,fd->tf", mlp_grad, down_weight, preferred_element_type=jnp.float32)
    slope = 0.5 * (1.0 + inner_tanh) + 0.5 * pre * (1.0 - inner_tanh * inner_tanh) * GELU_C * (
        1.0 + 3.0 * GELU_K * pre * pre
    )
    pre_grad = (act_grad * slope).astype(jnp.bfloat16)
    g_up_weight = jnp.einsum("td,tf->df", hidden2, pre_grad, preferred_element_type=jnp.float32)
    g_up_bias = jnp.sum(pre_grad.astype(jnp.float32), axis=0)
    hid2_grad = jnp.einsum(
        "tf,df->td", pre_grad, up_weight, preferred_element_type=jnp.float32
    ).reshape(frames_dev, PATCH, width)
    shift2_grad = jnp.sum(hid2_grad, axis=1)
    scale2_grad = jnp.sum(hid2_grad * normed2, axis=1)
    resid_grad = dy_grad + norm_back(hid2_grad * (1.0 + scale2), normed2, inv_std2)
    gate1_grad = jnp.sum(resid_grad * branch, axis=1)
    branch_grad = (gate1 * resid_grad).astype(jnp.bfloat16).reshape(tok_dev, width)
    g_proj_weight = jnp.einsum(
        "td,te->de", attn_tok, branch_grad, preferred_element_type=jnp.float32
    )
    g_proj_bias = jnp.sum(branch_grad.astype(jnp.float32), axis=0)
    attn_grad_tok = jnp.einsum(
        "te,de->td", branch_grad, proj_weight, preferred_element_type=jnp.float32
    ).astype(jnp.bfloat16)
    attn_grad = lax.all_to_all(
        attn_grad_tok, "uly", split_axis=1, concat_axis=0, tiled=True
    ).reshape(block_tok, heads_dev, DH)
    row_delta = jnp.einsum("qhd,qhd->hq", attn_grad.astype(jnp.float32), mixed_exact)

    def back_piece(query_acc, pieces):
        k_rows, v_rows, clip_k, time_k = pieces
        allowed, score = piece_score(k_rows, clip_k, time_k)
        prob = jnp.where(allowed[None], jnp.exp(score - log_total[..., None]), 0.0)
        prob_grad = jnp.einsum(
            "qhd,khd->hqk", attn_grad, v_rows, preferred_element_type=jnp.float32
        )
        score_grad = (prob * (prob_grad - row_delta[..., None])).astype(jnp.bfloat16)
        query_acc = (
            query_acc
            + jnp.einsum("hqk,khd->qhd", score_grad, k_rows, preferred_element_type=jnp.float32)
            * scale
        )
        key_rows = (
            jnp.einsum("hqk,qhd->khd", score_grad, queries, preferred_element_type=jnp.float32)
            * scale
        )
        value_rows = jnp.einsum(
            "hqk,qhd->khd", prob.astype(jnp.bfloat16), attn_grad, preferred_element_type=jnp.float32
        )
        return (query_acc, (key_rows, value_rows))

    query_grad, (key_terms, value_terms) = lax.scan(
        back_piece, zero_rows, (key_pieces, value_pieces, clip_pieces, time_pieces)
    )
    key_terms = key_terms.reshape(n_blk * block_tok, head_cols)
    value_terms = value_terms.reshape(n_blk * block_tok, head_cols)
    key_local, value_local = (
        lax.psum_scatter(
            key_terms.astype(jnp.bfloat16), "blk", scatter_dimension=0, tiled=True
        ).astype(jnp.float32),
        lax.psum_scatter(
            value_terms.astype(jnp.bfloat16), "blk", scatter_dimension=0, tiled=True
        ).astype(jnp.float32),
    )
    dq_heads = rotate(query_grad.reshape(block_tok, head_cols), cos_blk, sin_blk, -1.0).astype(
        jnp.bfloat16
    )
    dk_heads = rotate(key_local, cos_blk, sin_blk, -1.0).astype(jnp.bfloat16)
    dv_heads = value_local.astype(jnp.bfloat16)
    dq_tok, dk_tok, dv_tok = (
        lax.all_to_all(dq_heads, "uly", split_axis=0, concat_axis=1, tiled=True),
        lax.all_to_all(dk_heads, "uly", split_axis=0, concat_axis=1, tiled=True),
        lax.all_to_all(dv_heads, "uly", split_axis=0, concat_axis=1, tiled=True),
    )
    qkv_grad = jnp.concatenate([dq_tok, dk_tok, dv_tok], axis=1)
    g_attn_weight = jnp.einsum("td,te->de", hidden1, qkv_grad, preferred_element_type=jnp.float32)
    g_attn_bias = jnp.sum(qkv_grad.astype(jnp.float32), axis=0)
    hid1_grad = jnp.einsum(
        "te,de->td", qkv_grad, attn_weight, preferred_element_type=jnp.float32
    ).reshape(frames_dev, PATCH, width)
    shift1_grad = jnp.sum(hid1_grad, axis=1)
    scale1_grad = jnp.sum(hid1_grad * normed1, axis=1)
    token_grad = (resid_grad + norm_back(hid1_grad * (1.0 + scale1), normed1, inv_std1)).reshape(
        tok_dev, width
    )
    mod_grad = jnp.concatenate(
        [shift1_grad, scale1_grad, gate1_grad, shift2_grad, scale2_grad, gate2_grad], axis=1
    )
    g_mod_weight = jnp.einsum(
        "fd,fe->de",
        silu_noise.astype(jnp.float32),
        mod_grad,
        precision=lax.Precision.HIGHEST,
        preferred_element_type=jnp.float32,
    )
    g_mod_bias = jnp.sum(mod_grad, axis=0)
    (
        g_mod_weight,
        g_mod_bias,
        g_attn_weight,
        g_attn_bias,
        g_proj_weight,
        g_proj_bias,
        g_up_weight,
        g_up_bias,
        g_down_weight,
        g_down_bias,
    ) = (
        lax.psum_scatter(g_mod_weight, ("blk", "uly"), scatter_dimension=0, tiled=True),
        lax.psum_scatter(g_mod_bias, ("blk", "uly"), scatter_dimension=0, tiled=True),
        lax.psum_scatter(g_attn_weight, ("blk", "uly"), scatter_dimension=0, tiled=True),
        lax.psum_scatter(g_attn_bias, ("blk", "uly"), scatter_dimension=0, tiled=True),
        lax.psum_scatter(g_proj_weight, ("blk", "uly"), scatter_dimension=0, tiled=True),
        lax.psum_scatter(g_proj_bias, ("blk", "uly"), scatter_dimension=0, tiled=True),
        lax.psum_scatter(g_up_weight, ("blk", "uly"), scatter_dimension=0, tiled=True),
        lax.psum_scatter(g_up_bias, ("blk", "uly"), scatter_dimension=0, tiled=True),
        lax.psum_scatter(g_down_weight, ("blk", "uly"), scatter_dimension=0, tiled=True),
        lax.psum_scatter(g_down_bias, ("blk", "uly"), scatter_dimension=0, tiled=True),
    )
    return (
        output,
        token_grad,
        g_mod_weight,
        g_mod_bias,
        g_attn_weight,
        g_attn_bias,
        g_proj_weight,
        g_proj_bias,
        g_up_weight,
        g_up_bias,
        g_down_weight,
        g_down_bias,
    )


def solution(mesh):
    in_specs = (
        P(("blk", "uly"), None),
        P(("blk", "uly"), None),
        P(("blk", "uly"), None),
        P(),
        P(),
        P(),
        P(),
        P(),
        P(),
        P(),
        P(),
        P(),
        P(),
        P(),
        P(),
    )
    out_specs = (
        P(("blk", "uly"), None),
        P(("blk", "uly"), None),
        P(("blk", "uly"), None),
        P(("blk", "uly")),
        P(("blk", "uly"), None),
        P(("blk", "uly")),
        P(("blk", "uly"), None),
        P(("blk", "uly")),
        P(("blk", "uly"), None),
        P(("blk", "uly")),
        P(("blk", "uly"), None),
        P(("blk", "uly")),
    )
    return jax.shard_map(
        on_device, mesh=mesh, in_specs=in_specs, out_specs=out_specs, check_vma=False
    )
```

profile of v0, /device:TPU:0, one launch (start us, length us, event | category | flops | bytes accessed | tf_op | source)
XLA Modules:
  0.0 1709.3 jit_solution(14024680513358716793)
XLA Ops:
  44.5 11.9 all_to_all.131
  83.2 36.0 %all-gather.5.cloned.1.call-done = bf16[6400,256]{1,0:T(8,128)(2,1)} async-done(((bf16[800,256]{1,0:T(8,128)(2,1)}), bf16[6400,256]{1,0:T(8,128)(2,1)}) %all-gather.5.cloned.1.call-update) | async-done | bytes 3276816 | tf_op jit(solution)/shard_map/all_gather | solution.py:123
  139.9 112.5 %while.41 = (s32[]{:T(128)}, f32[4,800]{1,0:T(4,128)S(1)}, f32[4,800]{1,0:T(4,128)}, s32[4,1600]{1,0:T(4,128)S(1)}, s32[4,1600]{1,0:T(4,128)S(1)}, /*index=5*/bf...) while((s32[]{:T(128)}, f32[4,800]{1,0:T(4,128)S(1)}, ...), condition=%wide.region_5.6_spmd.clone, body=%wide.region_2.5_spmd.clone.sunk | while | flops 700176000 | bytes 46394932 | solution.py:157
  144.0 13.0 fusion.152
  172.3 12.9 fusion.152
  200.4 12.9 fusion.152
  228.4 12.9 fusion.152
  274.3 70.2 %while.42 = (s32[]{:T(128)}, f32[800,4,64]{0,2,1:T(8,128)}, f32[800,4,64]{0,2,1:T(8,128)S(1)}, bf16[4,1600,4,64]{1,3,2,0:T(8,128)(2,1)}, s32[4,1600]{1,0:T(4,128...) while((s32[]{:T(128)}, f32[800,4,64]{0,2,1:T(8,128)}, ...), condition=%wide.region_7.8_spmd.clone, body=%wide.region_6.7_spmd.clone.sunk | while | flops 1991219200 | bytes 60277552 | solution.py:176
  414.3 184.9 %while.43 = (s32[]{:T(128)}, f32[800,4,64]{0,2,1:T(8,128)S(1)}, bf16[4,1600,4,64]{1,3,2,0:T(8,128)(2,1)}, bf16[4,1600,4,64]{1,3,2,0:T(8,128)(2,1)}, bf16[4,1600,...) while((s32[]{:T(128)}, f32[800,4,64]{0,2,1:T(8,128)S(1)}, ...), condition=%wide.region_13.14_spmd.clone, body=%wide.region_12.13_spmd.clone.sunk | while | flops 3322624000 | bytes 147058464 | solution.py:252
  416.2 11.7 fusion.173
  437.7 12.5 fusion.174
  462.4 11.7 fusion.173
  483.9 12.5 fusion.174
  508.6 11.7 fusion.173
  530.0 12.5 fusion.174
  576.2 12.5 fusion.174
  646.5 48.1 %reduce-scatter.24.cloned.1.call-done = bf16[800,256]{1,0:T(8,128)(2,1)} async-done(((bf16[6400,256]{1,0:T(8,128)(2,1)}), bf16[800,256]{1,0:T(8,128)(2,1)}) %reduce-scatter.24.cloned.1.call-update) | async-done | bytes 409616 | tf_op jit(solution)/shard_map/reduce_scatter | solution.py:261
  698.0 75.6 %reduce-scatter.22.cloned.1.call-done = bf16[800,256]{1,0:T(8,128)(2,1)} async-done(((bf16[6400,256]{1,0:T(8,128)(2,1)}), bf16[800,256]{1,0:T(8,128)(2,1)}) %reduce-scatter.22.cloned.1.call-update) | async-done | bytes 409616
  863.3 13.4 fusion.79
  877.5 41.1 %all-reduce.5 = (f32[6144]{0:T(1024)S(1)}, f32[3072]{0:T(1024)S(1)}, f32[1024]{0:T(1024)S(1)}, f32[4096]{0:T(1024)S(1)}, f32[1024]{0:T(1024)S(1)}) all-reduce(f32[6144]{0:T(1024)S(1)} %reduce_sum.194, f32[3072]{0:T(1024)S(1)} %convert_reduce_fusion.1, f32[1024]{0:T(1024)S(1)} %copy-done.64, ...), channel_id=5, replica_groups=mesh['blk'=8,'uly'=4] {'blk','uly'}, use_global_device_ids=true, to_apply=%region_26.27.clone | all-reduce | flops 15360 | bytes 122880
  921.5 153.3 %reduce-scatter.14.cloned.1.call-done = f32[32,3072]{1,0:T(8,128)} async-done(((f32[1024,3072]{1,0:T(8,128)}), f32[32,3072]{1,0:T(8,128)}) %reduce-scatter.14.cloned.1.call-update) | async-done | bytes 393232 | tf_op jit(solution)/shard_map/reduce_scatter | solution.py:311
  1074.9 185.0 %reduce-scatter.20.cloned.1.call-done = f32[128,1024]{1,0:T(8,128)} async-done(((f32[4096,1024]{1,0:T(8,128)}), f32[128,1024]{1,0:T(8,128)}) %reduce-scatter.20.cloned.1.call-update) | async-done | bytes 524304 | tf_op jit(solution)/shard_map/reduce_scatter | solution.py:317
  1259.9 187.3 %reduce-scatter.18.cloned.1.call-done = f32[32,4096]{1,0:T(8,128)} async-done(((f32[1024,4096]{1,0:T(8,128)}), f32[32,4096]{1,0:T(8,128)}) %reduce-scatter.18.cloned.1.call-update) | async-done | bytes 524304 | tf_op jit(solution)/shard_map/reduce_scatter | solution.py:315
  1447.1 255.4 %reduce-scatter.12.cloned.1.call-done = f32[32,6144]{1,0:T(8,128)} async-done(((f32[1024,6144]{1,0:T(8,128)}), f32[32,6144]{1,0:T(8,128)}) %reduce-scatter.12.cloned.1.call-update) | async-done | bytes 786448 | tf_op jit(solution)/shard_map/reduce_scatter | solution.py:309
  (523 shorter events, 549.0 us)
Async XLA Ops:
  7.2 368.4 %copy-start = (bf16[1024,1024]{1,0:T(8,128)(2,1)S(1)}, bf16[1024,1024]{1,0:T(8,128)(2,1)}, u32[]{:S(2)}) copy-start(bf16[1024,1024]{1,0:T(8,128)(2,1)} %param.30) | copy-start | bytes 6291460
  7.2 112.1 %all-gather.5.cloned.1.call-start = ((), (), s32[]{:S(2)}) async-start(), calls=%async_computation.16 | async-start | bytes 3686400 | tf_op jit(solution)/shard_map/all_gather | solution.py:123
  7.3 29.8 %copy-start.71 = (f32[32]{0:T(128)}, f32[32]{0:T(128)S(1)}, u32[]{:S(2)}) copy-start(f32[32]{0:T(128)S(1)} %fusion.78) | copy-start | bytes 388
  7.3 29.7 %copy-start.73 = (pred[32]{0:T(512)(128)(4,1)}, pred[32]{0:T(512)(128)(4,1)S(1)}, u32[]{:S(2)}) copy-start(pred[32]{0:T(512)(128)(4,1)S(1)} %get-tuple-element.561) | copy-start | bytes 100
  7.3 29.7 %copy-start.75 = (pred[32]{0:T(512)(128)(4,1)}, pred[32]{0:T(512)(128)(4,1)S(1)}, u32[]{:S(2)}) copy-start(pred[32]{0:T(512)(128)(4,1)S(1)} %get-tuple-element.562) | copy-start | bytes 100
  60.4 11.1 all-to-all-start.2
  71.4 11.8 all-to-all-start
  75.5 176.8 %all-gather.3.cloned.1.call-start = ((), (), s32[]{:S(2)}) async-start(), calls=%async_computation.15 | async-start | bytes 3686400 | tf_op jit(solution)/shard_map/all_gather | solution.py:124
  351.2 23.2 %all-to-all-start.3 = ((bf16[4,200,256]{2,1,0:T(8,128)(2,1)}), bf16[4,200,256]{2,1,0:T(8,128)(2,1)}, u32[]{:S(2)}, u32[]{:S(2)}) async-start(bf16[4,200,256]{2,1,0:T(8,128)(2,1)} %copy.85), calls=%async_computation.3 | async-start | bytes 819200 | tf_op jit(solution)/shard_map/all_to_all | solution.py:180
  378.5 19.4 %copy-start.7 = (f32[200,1024]{1,0:T(8,128)}, f32[200,1024]{1,0:T(8,128)S(1)}, u32[]{:S(2)}) copy-start(f32[200,1024]{1,0:T(8,128)S(1)} %get-tuple-element.520) | copy-start | bytes 2457604
  378.5 19.4 %copy-start.52 = (f32[200]{0:T(256)}, f32[200]{0:T(256)S(1)}, u32[]{:S(2)}) copy-start(f32[200]{0:T(256)S(1)} %broadcast_multiply_fusion.4) | copy-start | bytes 2404
  401.3 11.1 all-to-all-start.4
  404.7 289.8 %reduce-scatter.24.cloned.1.call-start = ((), (), s32[]{:S(2)}) async-start(), calls=%async_computation.23 | async-start | bytes 3686400 | tf_op jit(solution)/shard_map/reduce_scatter | solution.py:261
  620.3 153.3 %reduce-scatter.22.cloned.1.call-start = ((), (), s32[]{:S(2)}) async-start(), calls=%async_computation.22 | async-start | bytes 3686400
  641.2 280.3 %reduce-scatter.16.cloned.1.call-start = ((), (), s32[]{:S(2)}) async-start(), calls=%async_computation.19 | async-start | bytes 4325376 | tf_op jit(solution)/shard_map/reduce_scatter | solution.py:313
  694.6 85.9 %all-to-all-start.7 = ((bf16[4,200,256]{2,1,0:T(8,128)(2,1)}), bf16[4,200,256]{2,1,0:T(8,128)(2,1)S(1)}, u32[]{:S(2)}, u32[]{:S(2)}) async-start(bf16[4,200,256]{2,1,0:T(8,128)(2,1)} %bitcast.231), calls=%async_computation.7 | async-start | bytes 819200 | tf_op jit(solution)/shard_map/all_to_all | solution.py:273
  780.4 12.8 all-to-all-start.6
  785.5 22.9 %copy-start.39 = (bf16[200,1024]{1,0:T(8,128)(2,1)S(1)}, bf16[200,1024]{1,0:T(8,128)(2,1)}, u32[]{:S(2)}) copy-start(bf16[200,1024]{1,0:T(8,128)(2,1)} %copy-done.38) | copy-start | bytes 1228804
  793.2 14.0 all-to-all-start.5
  796.7 278.1 %reduce-scatter.14.cloned.1.call-start = ((), (), s32[]{:S(2)}) async-start(), calls=%async_computation.18 | async-start | bytes 12976128 | tf_op jit(solution)/shard_map/reduce_scatter | solution.py:311
  814.8 445.1 %reduce-scatter.20.cloned.1.call-start = ((), (), s32[]{:S(2)}) async-start(), calls=%async_computation.21 | async-start | bytes 17301504 | tf_op jit(solution)/shard_map/reduce_scatter | solution.py:317
  826.0 621.1 %reduce-scatter.18.cloned.1.call-start = ((), (), s32[]{:S(2)}) async-start(), calls=%async_computation.20 | async-start | bytes 17301504 | tf_op jit(solution)/shard_map/reduce_scatter | solution.py:315
  835.8 866.8 %reduce-scatter.12.cloned.1.call-start = ((), (), s32[]{:S(2)}) async-start(), calls=%async_computation.17 | async-start | bytes 25952256 | tf_op jit(solution)/shard_map/reduce_scatter | solution.py:309
  876.8 825.8 %copy-start.1 = (bf16[1024,1024]{1,0:T(8,128)(2,1)S(1)}, bf16[1024,1024]{1,0:T(8,128)(2,1)}, u32[]{:S(2)}) copy-start(bf16[1024,1024]{1,0:T(8,128)(2,1)} %param.30) | copy-start | bytes 6291460
  (102 other events, 594.4 us)
Sparse Core Ops, SparseCore 0:
  56.5 62.7 all-gather.4
  121.4 60.4 all-gather.2
  620.4 74.0 reduce-scatter.23
  698.4 75.1 reduce-scatter.21
  776.3 140.2 reduce-scatter.15
  923.0 151.7 reduce-scatter.13
  1077.8 182.0 reduce-scatter.19
  1262.9 184.2 reduce-scatter.17
  1455.3 247.2 reduce-scatter.11
where the time goes:
time: 1720 us; the launch traced here: 1710 us
  waiting for transfers between devices  974 us (57%)
  matrix products  376 us (22%)
  local copies, waits for them, and re-layouts  170 us (10%)
  other arithmetic  93.1 us (5%)
  blocking collectives  53 us (3%)
  starting transfers between devices  26.5 us (2%)
    reduce_scatter x1, waiting for transfers between devices, on_device(): lax.psum_scatter(g_mod_weight, ('blk', 'uly'), scatter_dimension=0, tiled...  255 us
    reduce_scatter x1, waiting for transfers between devices, on_device(): lax.psum_scatter(g_up_weight, ('blk', 'uly'), scatter_dimension=0, tiled=...  187 us
    reduce_scatter x1, waiting for transfers between devices, on_device(): lax.psum_scatter(g_down_weight, ('blk', 'uly'), scatter_dimension=0, tile...  185 us
    reduce_scatter x1, waiting for transfers between devices, on_device(): lax.psum_scatter(g_attn_weight, ('blk', 'uly'), scatter_dimension=0, tile...  153 us
    dot_general x12, matrix products, piece_score(): jnp.einsum('qhd,khd->hqk', queries, k_rows, preferred_element_type=jnp.fl...  131 us
    unnamed x10, waiting for transfers between devices  75.7 us
    unnamed x175, local copies, waits for them, and re-layouts  73.7 us
    dot_general x4, matrix products, back_piece(): jnp.einsum('qhd,khd->hqk', attn_grad, v_rows, preferred_element_type=jnp....  50 us
  transfers between devices with their start and end apart: 16, of which 12 were waited for; matrix products, arithmetic and copies ran while one was open for 15% of the time, Pallas kernels for 0%

commit v1 on v0

--- a/solution.py
+++ b/solution.py
@@ -119,8 +119,39 @@
         lax.all_to_all(k_tok, "uly", split_axis=1, concat_axis=0, tiled=True),
         lax.all_to_all(v_tok, "uly", split_axis=1, concat_axis=0, tiled=True),
     )
+
+    def launch_matrix_all(inp):
+        axis_tag = "blk"
+        piece_now = lax.psum(1, axis_tag)
+        kept_arr = lax.axis_index(axis_tag)
+        before, then, moved = (piece_now, kept_arr, inp.shape[0])
+        lower = jnp.zeros(
+            [ix * before if idx == 0 else ix for idx, ix in enumerate(inp.shape)], inp.dtype
+        )
+        a_now = met_up = inp
+        after = lax.dynamic_update_slice_in_dim(lower, inp, then * moved, axis=0)
+        j0 = 1
+        while j0 < before // 2 + 1:
+            a_now = lax.ppermute(
+                a_now, axis_tag, [(idx, (idx + 1) % before) for idx in range(before)]
+            )
+            after = lax.dynamic_update_slice_in_dim(
+                after, a_now, (then - j0) % before * moved, axis=0
+            )
+            if 2 * j0 < before:
+                met_up = lax.ppermute(
+                    met_up,
+                    axis_name=axis_tag,
+                    perm=[(idx, (idx - 1) % before) for idx in range(before)],
+                )
+                after = lax.dynamic_update_slice_in_dim(
+                    after, met_up, (then + j0) % before * moved, axis=0
+                )
+            j0 += 1
+        return after
+
     k_every, v_every = (
-        lax.all_gather(k_heads, "blk", axis=0, tiled=True),
+        launch_matrix_all(k_heads),
         lax.all_gather(v_heads, "blk", axis=0, tiled=True),
     )
     group = 2

time: 1720 us -> 1820 us (1.058)
  matrix products: 376 us -> 427 us
  local copies, waits for them, and re-layouts: 170 us -> 214 us
    dynamic_update_slice x0 -> x8, local copies, waits for them, and re-layouts: none -> 46.2 us  [the longest x4 22.7 us: launch_matrix_all(): lax.dynamic_update_slice_in_dim(after, a_now, (then - j0) % before * move...]
    all_gather x1 -> x0, waiting for transfers between devices: 36 us -> none  [on_device(): lax.all_gather(k_heads, 'blk', axis=0, tiled=True)]
    ppermute x0 -> x7, waiting for transfers between devices: none -> 29 us  [the longest x4 28.9 us: launch_matrix_all(): lax.ppermute(a_now, axis_tag, [(idx, (idx + 1) % before) for idx in range...]
    unnamed x10 -> x9, waiting for transfers between devices: 75.7 us -> 49.7 us
    dot_general x4, matrix products: 13.3 us -> 34.8 us  [mix_values(): jnp.einsum('hqk,khd->qhd', prob, v_rows.astype(jnp.float32), preferred_el...]
    unnamed x175 -> x183, local copies, waits for them, and re-layouts: 73.7 us -> 67.4 us
  transfers between devices with their start and end apart: 16 -> 22, of which waited for: 12 -> 15; matrix products, arithmetic and copies ran while one was open for 15% -> 17% of each run, Pallas kernels for 0% -> 0%
where the time goes in v1:
time: 1820 us; the launch traced here: 1800 us
  waiting for transfers between devices  963 us (53%)
  matrix products  427 us (23%)
  local copies, waits for them, and re-layouts  214 us (12%)
  other arithmetic  87.3 us (5%)
  blocking collectives  51.5 us (3%)
  starting transfers between devices  42.5 us (2%)
    reduce_scatter x1, waiting for transfers between devices, on_device(): lax.psum_scatter(g_mod_weight, ('blk', 'uly'), scatter_dimension=0, tiled...  255 us
    reduce_scatter x1, waiting for transfers between devices, on_device(): lax.psum_scatter(g_down_weight, ('blk', 'uly'), scatter_dimension=0, tile...  187 us
    reduce_scatter x1, waiting for transfers between devices, on_device(): lax.psum_scatter(g_up_weight, ('blk', 'uly'), scatter_dimension=0, tiled=...  185 us
    reduce_scatter x1, waiting for transfers between devices, on_device(): lax.psum_scatter(g_attn_weight, ('blk', 'uly'), scatter_dimension=0, tile...  158 us
    dot_general x12, matrix products, piece_score(): jnp.einsum('qhd,khd->hqk', queries, k_rows, preferred_element_type=jnp.fl...  141 us
    unnamed x183, local copies, waits for them, and re-layouts  67.4 us
    reduce_scatter x1, waiting for transfers between devices, on_device(): lax.psum_scatter(value_terms.astype(jnp.bfloat16), 'blk', scatter_dimensi...  57.7 us
    dot_general x4, matrix products, back_piece(): jnp.einsum('qhd,khd->hqk', attn_grad, v_rows, preferred_element_type=jnp....  50 us
  transfers between devices with their start and end apart: 22, of which 15 were waited for; matrix products, arithmetic and copies ran while one was open for 17% of the time, Pallas kernels for 0%

profile of v1, /device:TPU:0, one launch (start us, length us, event | category | flops | bytes accessed | tf_op | source)
XLA Modules:
  0.0 1803.3 jit_solution(15143291625145347449)
XLA Ops:
  61.8 14.5 collective-permute-done
  81.9 13.7 collective-permute-done.2
  194.4 100.5 %while.41 = (s32[]{:T(128)}, f32[4,800]{1,0:T(4,128)S(1)}, f32[4,800]{1,0:T(4,128)S(1)}, s32[4,1600]{1,0:T(4,128)S(1)}, s32[4,1600]{1,0:T(4,128)S(1)}, /*index=5...) while((s32[]{:T(128)}, f32[4,800]{1,0:T(4,128)S(1)}, ...), condition=%wide.region_5.6_spmd.clone, body=%wide.region_2.5_spmd.clone.sunk | while | flops 700176000 | bytes 46341816 | solution.py:188
  196.5 13.0 fusion.152
  221.5 12.9 fusion.152
  246.5 12.9 fusion.152
  271.5 12.9 fusion.152
  316.2 114.2 %while.42 = (s32[]{:T(128)}, f32[800,4,64]{0,2,1:T(8,128)S(1)}, f32[800,4,64]{0,2,1:T(8,128)}, bf16[4,1600,4,64]{1,3,2,0:T(8,128)(2,1)}, s32[4,1600]{1,0:T(4,128...) while((s32[]{:T(128)}, f32[800,4,64]{0,2,1:T(8,128)S(1)}, ...), condition=%wide.region_7.8_spmd.clone, body=%wide.region_6.7_spmd.clone.sunk | while | flops 1991219200 | bytes 81070936 | solution.py:207
  492.1 200.4 %while.43 = (s32[]{:T(128)}, f32[800,4,64]{0,2,1:T(8,128)S(1)}, bf16[4,1600,4,64]{1,3,2,0:T(8,128)(2,1)}, bf16[4,1600,4,64]{1,3,2,0:T(8,128)(2,1)}, bf16[4,1600,...) while((s32[]{:T(128)}, f32[800,4,64]{0,2,1:T(8,128)S(1)}, ...), condition=%wide.region_13.14_spmd.clone, body=%wide.region_12.13_spmd.clone.sunk | while | flops 3322624000 | bytes 106510560 | solution.py:283
  506.0 12.5 fusion.174
  544.2 11.7 fusion.173
  556.0 12.5 fusion.174
  594.2 11.7 fusion.173
  606.0 12.5 fusion.174
  656.0 12.5 fusion.174
  739.5 49.5 %reduce-scatter.22.cloned.1.call-done = bf16[800,256]{1,0:T(8,128)(2,1)} async-done(((bf16[6400,256]{1,0:T(8,128)(2,1)}), bf16[800,256]{1,0:T(8,128)(2,1)}) %reduce-scatter.22.cloned.1.call-update) | async-done | bytes 409616
  810.4 57.7 %reduce-scatter.24.cloned.1.call-done = bf16[800,256]{1,0:T(8,128)(2,1)} async-done(((bf16[6400,256]{1,0:T(8,128)(2,1)}), bf16[800,256]{1,0:T(8,128)(2,1)}) %reduce-scatter.24.cloned.1.call-update) | async-done | bytes 409616 | tf_op jit(solution)/shard_map/reduce_scatter | solution.py:292
  937.8 13.4 fusion.79
  951.9 39.9 %all-reduce.5 = (f32[6144]{0:T(1024)S(1)}, f32[3072]{0:T(1024)S(1)}, f32[1024]{0:T(1024)S(1)}, f32[4096]{0:T(1024)S(1)}, f32[1024]{0:T(1024)S(1)}) all-reduce(f32[6144]{0:T(1024)S(1)} %reduce_sum.194, f32[3072]{0:T(1024)S(1)} %convert_reduce_fusion.1, f32[1024]{0:T(1024)S(1)} %copy-done.63, ...), channel_id=5, replica_groups=mesh['blk'=8,'uly'=4] {'blk','uly'}, use_global_device_ids=true, to_apply=%region_26.27.clone | all-reduce | flops 15360 | bytes 122880
  994.8 15.9 reduce-scatter.16.cloned.1.call-done
  1010.7 157.8 %reduce-scatter.14.cloned.1.call-done = f32[32,3072]{1,0:T(8,128)} async-done(((f32[1024,3072]{1,0:T(8,128)}), f32[32,3072]{1,0:T(8,128)}) %reduce-scatter.14.cloned.1.call-update) | async-done | bytes 393232 | tf_op jit(solution)/shard_map/reduce_scatter | solution.py:342
  1168.5 184.7 %reduce-scatter.18.cloned.1.call-done = f32[32,4096]{1,0:T(8,128)} async-done(((f32[1024,4096]{1,0:T(8,128)}), f32[32,4096]{1,0:T(8,128)}) %reduce-scatter.18.cloned.1.call-update) | async-done | bytes 524304 | tf_op jit(solution)/shard_map/reduce_scatter | solution.py:346
  1353.3 187.5 %reduce-scatter.20.cloned.1.call-done = f32[128,1024]{1,0:T(8,128)} async-done(((f32[4096,1024]{1,0:T(8,128)}), f32[128,1024]{1,0:T(8,128)}) %reduce-scatter.20.cloned.1.call-update) | async-done | bytes 524304 | tf_op jit(solution)/shard_map/reduce_scatter | solution.py:348
  1540.8 255.3 %reduce-scatter.12.cloned.1.call-done = f32[32,6144]{1,0:T(8,128)} async-done(((f32[1024,6144]{1,0:T(8,128)}), f32[32,6144]{1,0:T(8,128)}) %reduce-scatter.12.cloned.1.call-update) | async-done | bytes 786448 | tf_op jit(solution)/shard_map/reduce_scatter | solution.py:340
  (535 shorter events, 670.5 us)
Async XLA Ops:
  7.2 446.3 %copy-start = (bf16[1024,1024]{1,0:T(8,128)(2,1)S(1)}, bf16[1024,1024]{1,0:T(8,128)(2,1)}, u32[]{:S(2)}) copy-start(bf16[1024,1024]{1,0:T(8,128)(2,1)} %param.30) | copy-start | bytes 6291460
  57.1 19.2 %collective-permute-start = (bf16[800,256]{1,0:T(8,128)(2,1)S(1)}, bf16[800,256]{1,0:T(8,128)(2,1)S(1)}, u32[]{:S(2)}, u32[]{:S(2)}) collective-permute-start(bf16[800,256]{1,0:T(8,128)(2,1)S(1)} %bitcast.224), channel_id=1, source_target_pairs={{0,4},{4,8},{8,12},{12,16},{16,20},{20,24},{24,28},{28,0},{1,5},{5... | collective-permute-start | bytes 1228808 | tf_op jit(solution)/shard_map/ppermute | solution.py:135
  58.6 20.2 %collective-permute-start.1 = (bf16[800,256]{1,0:T(8,128)(2,1)S(1)}, bf16[800,256]{1,0:T(8,128)(2,1)S(1)}, u32[]{:S(2)}, u32[]{:S(2)}) collective-permute-start(bf16[800,256]{1,0:T(8,128)(2,1)S(1)} %bitcast.225), channel_id=1, source_target_pairs={{0,28},{4,0},{8,4},{12,8},{16,12},{20,16},{24,20},{28,24},{1,29},{... | collective-permute-start | bytes 1228808 | tf_op jit(solution)/shard_map/ppermute | solution.py:142
  76.3 19.3 %collective-permute-start.2 = (bf16[800,256]{1,0:T(8,128)(2,1)S(1)}, bf16[800,256]{1,0:T(8,128)(2,1)}, u32[]{:S(2)}, u32[]{:S(2)}) collective-permute-start(bf16[800,256]{1,0:T(8,128)(2,1)S(1)} %collective-permute-done), channel_id=1, source_target_pairs={{0,4},{4,8},{8,12},{12,16},{16,20},{20,24},{24,28},{28,0},{1,5},{5... | collective-permute-start | bytes 1228808 | tf_op jit(solution)/shard_map/ppermute | solution.py:135
  78.8 27.1 %collective-permute-start.3 = (bf16[800,256]{1,0:T(8,128)(2,1)S(1)}, bf16[800,256]{1,0:T(8,128)(2,1)}, u32[]{:S(2)}, u32[]{:S(2)}) collective-permute-start(bf16[800,256]{1,0:T(8,128)(2,1)S(1)} %collective-permute-done.1), channel_id=1, source_target_pairs={{0,28},{4,0},{8,4},{12,8},{16,12},{20,16},{24,20},{28,24},{1,29},{... | collective-permute-start | bytes 1228808 | tf_op jit(solution)/shard_map/ppermute | solution.py:142
  95.6 14.1 collective-permute-start.4
  102.4 11.1 all-to-all-start.2
  105.9 62.4 %collective-permute-start.5 = (bf16[800,256]{1,0:T(8,128)(2,1)}, bf16[800,256]{1,0:T(8,128)(2,1)}, u32[]{:S(2)}, u32[]{:S(2)}) collective-permute-start(bf16[800,256]{1,0:T(8,128)(2,1)} %collective-permute-done.3), channel_id=1, source_target_pairs={{0,28},{4,0},{8,4},{12,8},{16,12},{20,16},{24,20},{28,24},{1,29},{... | collective-permute-start | bytes 1228808 | tf_op jit(solution)/shard_map/ppermute | solution.py:142
  109.7 65.8 %collective-permute-start.6 = (bf16[800,256]{1,0:T(8,128)(2,1)}, bf16[800,256]{1,0:T(8,128)(2,1)}, u32[]{:S(2)}, u32[]{:S(2)}) collective-permute-start(bf16[800,256]{1,0:T(8,128)(2,1)} %collective-permute-done.4), channel_id=1, source_target_pairs={{0,4},{4,8},{8,12},{12,16},{16,20},{20,24},{24,28},{28,0},{1,5},{5... | collective-permute-start | bytes 1228808 | tf_op jit(solution)/shard_map/ppermute | solution.py:135
  113.5 11.8 all-to-all-start
  117.6 177.9 %all-gather.2.cloned.1.call-start = ((), (), s32[]{:S(2)}) async-start(), calls=%async_computation.15 | async-start | bytes 3686400 | tf_op jit(solution)/shard_map/all_gather | solution.py:155
  433.9 18.4 %all-to-all-start.3 = ((bf16[4,200,256]{2,1,0:T(8,128)(2,1)}), bf16[4,200,256]{2,1,0:T(8,128)(2,1)}, u32[]{:S(2)}, u32[]{:S(2)}) async-start(bf16[4,200,256]{2,1,0:T(8,128)(2,1)} %copy.106), calls=%async_computation.3 | async-start | bytes 819200 | tf_op jit(solution)/shard_map/all_to_all | solution.py:211
  479.1 11.1 all-to-all-start.4
  482.6 306.5 %reduce-scatter.22.cloned.1.call-start = ((), (), s32[]{:S(2)}) async-start(), calls=%async_computation.21 | async-start | bytes 3686400
  713.4 154.7 %reduce-scatter.24.cloned.1.call-start = ((), (), s32[]{:S(2)}) async-start(), calls=%async_computation.22 | async-start | bytes 3686400 | tf_op jit(solution)/shard_map/reduce_scatter | solution.py:292
  734.2 276.5 %reduce-scatter.16.cloned.1.call-start = ((), (), s32[]{:S(2)}) async-start(), calls=%async_computation.18 | async-start | bytes 4325376 | tf_op jit(solution)/shard_map/reduce_scatter | solution.py:344
  795.8 11.1 all-to-all-start.6
  806.9 61.2 %all-to-all-start.5 = ((bf16[4,200,256]{2,1,0:T(8,128)(2,1)}), bf16[4,200,256]{2,1,0:T(8,128)(2,1)S(1)}, u32[]{:S(2)}, u32[]{:S(2)}) async-start(bf16[4,200,256]{2,1,0:T(8,128)(2,1)} %copy.112), calls=%async_computation.5 | async-start | bytes 819200 | tf_op jit(solution)/shard_map/all_to_all | solution.py:302
  868.1 12.5 all-to-all-start.7
  871.6 297.0 %reduce-scatter.14.cloned.1.call-start = ((), (), s32[]{:S(2)}) async-start(), calls=%async_computation.17 | async-start | bytes 12976128 | tf_op jit(solution)/shard_map/reduce_scatter | solution.py:342
  888.1 465.1 %reduce-scatter.18.cloned.1.call-start = ((), (), s32[]{:S(2)}) async-start(), calls=%async_computation.19 | async-start | bytes 17301504 | tf_op jit(solution)/shard_map/reduce_scatter | solution.py:346
  897.8 643.0 %reduce-scatter.20.cloned.1.call-start = ((), (), s32[]{:S(2)}) async-start(), calls=%async_computation.20 | async-start | bytes 17301504 | tf_op jit(solution)/shard_map/reduce_scatter | solution.py:348
  909.1 887.0 %reduce-scatter.12.cloned.1.call-start = ((), (), s32[]{:S(2)}) async-start(), calls=%async_computation.16 | async-start | bytes 25952256 | tf_op jit(solution)/shard_map/reduce_scatter | solution.py:340
  951.2 844.8 %copy-start.1 = (bf16[1024,1024]{1,0:T(8,128)(2,1)S(1)}, bf16[1024,1024]{1,0:T(8,128)(2,1)}, u32[]{:S(2)}) copy-start(bf16[1024,1024]{1,0:T(8,128)(2,1)} %param.30) | copy-start | bytes 6291460
  (100 other events, 804.4 us)
Sparse Core Ops, SparseCore 0:
  125.4 61.3 all-gather.1
  713.5 75.4 reduce-scatter.21
  793.0 75.0 reduce-scatter.23
  870.8 139.8 reduce-scatter.15
  1017.2 151.3 reduce-scatter.13
  1171.4 181.8 reduce-scatter.17
  1356.2 184.4 reduce-scatter.19
  1548.9 247.1 reduce-scatter.11
